TPU v7x, 256 devices: a whole 4x4x8 slice. The times are simulated.
256 devices in a mesh: star: 64 (over y, z_lo, x, core), gas: 4 (over z_hi).
Axes of the slice: x: 4, y: 4, z: 8 (z_hi: 4, z_lo: 2; z = z_hi * 2 + z_lo), core: 2. Of those that a mesh axis runs over, the one named last changes fastest.
Arguments:
- star_pos: float32 [3, 131072], P(None, ('star', 'gas')), may hold values from 0 to 32
- star_vel: float32 [3, 131072], P(None, ('star', 'gas')), may hold values from -6 to 6
- star_accel: float32 [6, 131072], P(None, ('star', 'gas')), may hold values from -6 to 6
- star_mass: float32 [131072], P(('star', 'gas')), may hold values from 0.1 to 2
- active: int32 [2048], replicated, may hold values from 0 to 131071, as said below
- density: float32 [256, 32, 64], P('star', 'gas'), may hold values from 0.5 to 4
- flow_in: float32 [3, 256, 32, 64], P(None, 'star', 'gas'), may hold values from -2 to 2
- field_in: float32 [3, 256, 32, 64], P(None, 'star', 'gas'), may hold values from -4 to 4
Outputs:
- star_new: float32 [12, 131072], P(None, ('star', 'gas'))
- flow: float32 [3, 256, 32, 64], P(None, 'star', 'gas')
- field_out: float32 [3, 256, 32, 64], P(None, 'star', 'gas')
Inputs may be any that keep to these rules, and one draw needn't show every extreme that they name: Distinct and increasing; among the 512 consecutive indices of one device at most 24 are active, and in every draw some device holds exactly 24.
All inputs are finite; a program needn't handle non-finite values.
Results may differ from a plain program's by a relative error of at most 0.0001.
Values sent between devices are 32-bit elements; how exact they have to be, the bound alone decides.
A program may use at most 64 MiB of HBM per device.

v0:
```python
import math
import jax
import jax.numpy as jnp
from jax import lax
from jax.sharding import PartitionSpec as P

MOST = 24
gravity = 0.02
soften = 4.0
time_step = 1.5
field_step = 0.1
highest = lax.Precision.HIGHEST


def with_halo(block, sides, width):
    for axis, dim in sides:
        count = lax.axis_size(axis)
        forward = [(i, i + 1) for i in range(count - 1)]
        forward.append((count - 1, 0))
        backward = [(target, source) for source, target in forward]
        low = lax.ppermute(
            lax.slice_in_dim(block, block.shape[dim] - width, None, axis=dim), axis, forward
        )
        high = lax.ppermute(lax.slice_in_dim(block, 0, width, axis=dim), axis, backward)
        block = jnp.concatenate([low, block, high], axis=dim)
    return block


def grad_x(values):
    return 0.5 * (values[2:, 1:-1] - values[:-2, 1:-1])


def grad_y(values):
    return 0.5 * (values[1:-1, 2:] - values[1:-1, :-2])


def grad_z(values):
    return 0.5 * (jnp.roll(values, -1, 2) - jnp.roll(values, 1, 2))[1:-1, 1:-1]


def trim_rim(values):
    return values[1:-1, 1:-1]


def curl_of(comp_a, comp_b, comp_c):
    return (
        grad_y(comp_c) - grad_z(comp_b),
        grad_z(comp_a) - grad_x(comp_c),
        grad_x(comp_b) - grad_y(comp_a),
    )


def cross_of(lhs_vec, rhs_vec):
    return (
        lhs_vec[1] * rhs_vec[2] - lhs_vec[2] * rhs_vec[1],
        lhs_vec[2] * rhs_vec[0] - lhs_vec[0] * rhs_vec[2],
        lhs_vec[0] * rhs_vec[1] - lhs_vec[1] * rhs_vec[0],
    )


def field_rate(padded_field, padded_flow, padded_density):
    current = curl_of(padded_field[0], padded_field[1], padded_field[2])
    inner_field = (trim_rim(padded_field[0]), trim_rim(padded_field[1]), trim_rim(padded_field[2]))
    inner_flow = (trim_rim(padded_flow[0]), trim_rim(padded_flow[1]), trim_rim(padded_flow[2]))
    resist = trim_rim(padded_density) ** (-1.5)
    lorentz = cross_of(current, inner_field)
    drift = cross_of(lorentz, inner_field)
    motion = cross_of(inner_flow, inner_field)
    emf_a = motion[0] + resist * drift[0]
    emf_b = motion[1] + resist * drift[1]
    emf_c = motion[2] + resist * drift[2]
    return jnp.stack(curl_of(emf_a, emf_b, emf_c))


def pair_terms(target, resident, cell_place, cell_mass):
    star_gap = resident[0:3, None, :] - target[0:3, :, None]
    rel_vel = resident[3:6, None, :] - target[3:6, :, None]
    inv_r = lax.rsqrt(jnp.sum(star_gap * star_gap, 0) + soften)
    weight = gravity * resident[6][None, :] * inv_r * inv_r * inv_r
    star_acc = jnp.sum(weight[None] * star_gap, 2)
    approach = jnp.sum(star_gap * rel_vel, 0)
    star_jerk = jnp.sum(
        weight[None] * (rel_vel - 3.0 * (approach * inv_r * inv_r)[None] * star_gap), 2
    )
    cell_gap = cell_place[:, None, :] - target[0:3, :, None]
    inv_g = lax.rsqrt(jnp.sum(cell_gap * cell_gap, 0) + soften)
    inv_cube = gravity * inv_g * inv_g * inv_g
    gas_acc = jnp.sum((inv_cube * cell_mass[None, :])[None] * cell_gap, 2)
    cell_kick = -jnp.sum((inv_cube * target[6][:, None])[None] * cell_gap, 1)
    return (jnp.concatenate([star_acc + gas_acc, star_jerk], 0), cell_kick)


def all_terms(targets, resident, cell_place, cell_mass):
    target_total = targets.shape[1]
    block_width = math.gcd(target_total, 64)
    blocks = targets.reshape(7, target_total // block_width, block_width).transpose(1, 0, 2)

    def one_block(running, target_block):
        terms_here, cell_kick = pair_terms(target_block, resident, cell_place, cell_mass)
        return (running + cell_kick, terms_here)

    kick_sum, block_terms = lax.scan(one_block, jnp.zeros(cell_place.shape, jnp.float32), blocks)
    return (block_terms.transpose(1, 0, 2).reshape(6, target_total), kick_sum)


def body(star_pos, star_vel, star_accel, star_mass, active, density, flow_in, field_in):
    resident_total = star_pos.shape[1]
    old_acc = star_accel[0:3]
    old_jerk = star_accel[3:6]
    pred_pos = (
        star_pos
        + time_step * star_vel
        + time_step**2 / 2.0 * old_acc
        + time_step**3 / 6.0 * old_jerk
    )
    pred_vel = star_vel + time_step * old_acc + time_step**2 / 2.0 * old_jerk
    resident = jnp.concatenate([pred_pos, pred_vel, star_mass[None]], 0)
    my_rank = lax.axis_index("star") * lax.axis_size("gas") + lax.axis_index("gas")
    owner_of = active // resident_total
    local_slot = active % resident_total
    is_mine = owner_of == my_rank
    rows_iota = jnp.arange(resident_total, dtype=jnp.int32)
    owned = (is_mine[None, :] & (local_slot[None, :] == rows_iota[:, None])).astype(jnp.float32)
    active_mask = jnp.sum(owned, 1) > 0.5
    ext_x, ext_y, ext_z = density.shape
    grid_shape = (ext_x, ext_y, ext_z)
    coord_x = (lax.axis_index("star") * ext_x + jnp.arange(ext_x)).astype(jnp.float32) + 0.5
    coord_y = (lax.axis_index("gas") * ext_y + jnp.arange(ext_y)).astype(jnp.float32) + 0.5
    coord_z = jnp.arange(ext_z).astype(jnp.float32) + 0.5
    cell_place = jnp.stack(
        [
            jnp.broadcast_to(coord_x[:, None, None], grid_shape),
            jnp.broadcast_to(coord_y[None, :, None], grid_shape),
            jnp.broadcast_to(coord_z[None, None, :], grid_shape),
        ]
    ).reshape(3, -1)
    cell_mass = density.reshape(-1)
    order_rank = jnp.cumsum(is_mine.astype(jnp.int32)) - 1
    slot_iota = jnp.arange(MOST, dtype=jnp.int32)
    slot_pick = (is_mine[:, None] & (order_rank[:, None] == slot_iota[None, :])).astype(jnp.float32)
    selector = jnp.dot(owned, slot_pick, precision=highest)
    packed = jnp.dot(resident, selector, precision=highest)
    targets = lax.all_gather(packed, ("star", "gas"), axis=1, tiled=True)
    partial_terms, kick_sum = all_terms(targets, resident, cell_place, cell_mass)
    summed = lax.psum(partial_terms, ("star", "gas"))
    mine_terms = lax.dynamic_slice_in_dim(summed, my_rank * MOST, MOST, 1)
    own_terms = jnp.dot(mine_terms, selector.T, precision=highest)
    new_acc = own_terms[0:3]
    new_jerk = own_terms[3:6]
    vel_one = (
        star_vel
        + time_step * (old_acc + new_acc) / 2.0
        + time_step**2 * (old_jerk - new_jerk) / 12.0
    )
    pos_one = (
        star_pos
        + time_step * (star_vel + vel_one) / 2.0
        + time_step**2 * (old_acc - new_acc) / 12.0
    )
    updated = jnp.concatenate([pos_one, vel_one, new_acc, new_jerk], 0)
    base = jnp.concatenate([star_pos, star_vel, star_accel], 0)
    star_new = jnp.where(active_mask[None, :], updated, base)
    flow = flow_in + time_step * kick_sum.reshape(3, ext_x, ext_y, ext_z)

    def rate_of(values):
        padded = with_halo(
            jnp.concatenate([values, flow, density[None]], 0), (("star", 1), ("gas", 2)), 2
        )
        return field_rate(padded[0:3], padded[3:6], padded[6])

    first_section = field_in + field_step * rate_of(field_in)
    field_out = 0.5 * (field_in + first_section + field_step * rate_of(first_section))
    return (star_new, flow, field_out)


def solution(mesh):
    placed = (
        P(None, ("star", "gas")),
        P(None, ("star", "gas")),
        P(None, ("star", "gas")),
        P(("star", "gas")),
        P(),
        P("star", "gas", None),
        P(None, "star", "gas", None),
        P(None, "star", "gas", None),
    )
    return jax.shard_map(
        body,
        mesh=mesh,
        in_specs=placed,
        out_specs=(
            P(None, ("star", "gas")),
            P(None, "star", "gas", None),
            P(None, "star", "gas", None),
        ),
        check_vma=False,
    )
```

profile of v0, /device:TPU:1, one launch (start us, length us, event | category | flops | bytes accessed | tf_op | source)
XLA Modules:
  0.0 1057.4 jit_solution(8387592304197424626)
XLA Ops:
  7.3 0.7 add_select_fusion
  8.0 0.7 convert_bitcast_fusion
  9.3 1.4 fusion.14
  10.9 629.3 %all-gather = f32[256,24,7]{1,2,0:T(8,128)S(1)} all-gather(f32[1,24,7]{1,2,0:T(8,128)S(1)} %convolution_bitcast_fusion), channel_id=1, replica_groups=mesh['star'=64,'gas'=4] {'star','gas'}, dimensions={0}, use_global_device_ids=true | all-gather | bytes 172704 | tf_op jit(solution)/shard_map/all_gather | solution.py:143
  640.4 0.5 reshape.159
  641.8 144.5 %while.14 = (s32[]{:T(128)}, f32[3,2048]{1,0:T(4,128)S(1)}, f32[96,6,64]{2,1,0:T(8,128)S(1)}, f32[3,4,8,64]{3,2,1,0:T(8,128)}, f32[96,7,64]{2,0,1:T(8,128)S(1)},...) while((s32[]{:T(128)}, f32[3,2048]{1,0:T(4,128)S(1)}, ...), condition=%wide.wide.region_11.12_spmd.clone, body=%wide.wide.region_3.11_spmd.clone.sunk | while | flops 5353989 | bytes 4405187 | solution.py:102
  642.8 0.5 fusion.148
  644.3 0.5 fusion.148
  645.8 0.5 fusion.148
  647.3 0.5 fusion.148
  648.8 0.5 fusion.148
  650.3 0.5 fusion.148
  651.8 0.5 fusion.148
  653.3 0.5 fusion.148
  654.8 0.5 fusion.148
  656.3 0.5 fusion.148
  657.8 0.5 fusion.148
  659.3 0.5 fusion.148
  660.8 0.5 fusion.148
  662.3 0.5 fusion.148
  663.8 0.5 fusion.148
  666.8 0.5 fusion.148
  668.3 0.5 fusion.148
  669.9 0.5 fusion.148
  671.4 0.5 fusion.148
  672.9 0.5 fusion.148
  674.4 0.5 fusion.148
  675.9 0.5 fusion.148
  677.4 0.5 fusion.148
  678.9 0.5 fusion.148
  680.4 0.5 fusion.148
  681.9 0.5 fusion.148
  683.4 0.5 fusion.148
  684.9 0.5 fusion.148
  786.5 0.7 pad_maximum_fusion.9
  787.4 6.9 collective-permute-start.1
  794.3 0.8 reshape.156
  795.1 0.8 convert_reduce_fusion
  796.1 3.6 collective-permute-start.3
  799.7 1.9 collective-permute-done.2
  802.8 7.0 collective-permute-start.5
  809.8 231.5 %all-reduce.2.cloned.1.call-done = f32[6,6144]{1,0:T(8,128)} async-done(((f32[6,6144]{1,0:T(8,128)}), f32[6,6144]{1,0:T(8,128)}) %all-reduce.2.cloned.1.call-update) | async-done | bytes 147472 | tf_op jit(solution)/shard_map/psum | solution.py:145
  1041.2 0.9 fusion.97
  1042.2 0.9 collective-permute-start.6
  1043.1 2.7 collective-permute-start.7
  1045.9 0.6 maximum_select_fusion
  1046.5 2.1 collective-permute-done.6
  1049.9 0.6 fusion.58
  (1313 shorter events, 127.1 us)
Async XLA Ops:
  7.2 1034.1 %all-reduce.2.cloned.1.call-start = ((), (), s32[]{:S(2)}) async-start(), calls=%async_computation | async-start | bytes 393216 | tf_op jit(solution)/shard_map/psum | solution.py:145
  9.3 1.4 copy-start.5
  9.3 1.4 copy-start.7
  9.3 1.4 copy-start.8
  9.3 1.5 copy-start.6
  640.3 1.0 copy-start.2
  641.2 0.6 copy-start.4
  641.8 144.7 %copy-start.9 = (f32[3,4,8,64]{3,2,1,0:T(8,128)S(1)}, f32[3,4,8,64]{3,2,1,0:T(8,128)}, u32[]{:S(2)}) copy-start(f32[3,4,8,64]{3,2,1,0:T(8,128)} %param.16) | copy-start | bytes 73732
  641.8 144.7 %copy-start.1 = (f32[3,4,8,64]{3,2,1,0:T(8,128)S(1)}, f32[3,4,8,64]{3,2,1,0:T(8,128)}, u32[]{:S(2)}) copy-start(f32[3,4,8,64]{3,2,1,0:T(8,128)} %param.17) | copy-start | bytes 73732
  786.4 9.5 copy-start.3
  786.5 262.1 %copy-start = (f32[3,4,8,64]{3,2,1,0:T(8,128)}, f32[3,4,8,64]{3,2,1,0:T(8,128)S(1)}, u32[]{:S(2)}) copy-start(f32[3,4,8,64]{3,2,1,0:T(8,128)S(1)} %add.174) | copy-start | bytes 73732
  787.3 8.6 collective-permute-start
  787.4 8.5 collective-permute-start.1
  796.0 5.5 collective-permute-start.2
  796.1 5.4 collective-permute-start.3
  802.7 239.5 %collective-permute-start.4 = (f32[7,2,8,64]{3,2,1,0:T(8,128)S(1)}, f32[7,2,8,64]{3,2,1,0:T(8,128)S(1)}, u32[]{:S(2)}, u32[]{:S(2)}) collective-permute-start(f32[7,2,8,64]{3,2,1,0:T(8,128)S(1)} %get-tuple-element.178), channel_id=1, source_target_pairs={{0,4},{4,8},{8,12},{12,16},{16,20},{20,24},{24,28},{28,32},{32,36}... | collective-permute-start | bytes 86024 | tf_op jit(solution)/shard_map/ppermute | solution.py:21
  802.8 239.4 %collective-permute-start.5 = (f32[7,2,8,64]{3,2,1,0:T(8,128)S(1)}, f32[7,2,8,64]{3,2,1,0:T(8,128)S(1)}, u32[]{:S(2)}, u32[]{:S(2)}) collective-permute-start(f32[7,2,8,64]{3,2,1,0:T(8,128)S(1)} %get-tuple-element.179), channel_id=1, source_target_pairs={{4,0},{8,4},{12,8},{16,12},{20,16},{24,20},{28,24},{32,28},{36,32}... | collective-permute-start | bytes 86024 | tf_op jit(solution)/shard_map/ppermute | solution.py:24
  1042.2 6.4 collective-permute-start.6
  1043.1 5.5 collective-permute-start.7
Sparse Core Ops, SparseCore 0:
  795.3 245.9 all-reduce.1
where the time goes:
time: 1060 us
  blocking collectives  629 us (59%)
  waiting for transfers between devices  235 us (22%)
  other arithmetic  139 us (13%)
  starting transfers between devices  21.4 us (2%)
  between operations  14.4 us (1%)
    all_gather x1, blocking collectives, body(): targets = lax.all_gather(packed, ('star', 'gas'), axis=1, tiled=True)  629 us
    psum x1, waiting for transfers between devices, body(): summed = lax.psum(partial_terms, ('star', 'gas'))  231 us
    reduce_sum x96, other arithmetic, pair_terms(): gas_acc = jnp.sum((inv_cube * cell_mass[None, :])[None] * cell_gap, 2)  48.2 us
    reduce_sum x96, other arithmetic, pair_terms(): star_acc = jnp.sum(weight[None] * star_gap, 2)  27.3 us
  transfers between devices with their start and end apart: 9, of which 3 were waited for; matrix products, arithmetic and copies ran while one was open for 0% of the time, Pallas kernels for 0%

commit v1 on v0

--- a/solution.py
+++ b/solution.py
@@ -3,6 +3,7 @@
 import jax.numpy as jnp
 from jax import lax
 from jax.sharding import PartitionSpec as P
+from jax.lax import all_gather
 
 MOST = 24
 gravity = 0.02
@@ -104,6 +105,12 @@
 
 
 def body(star_pos, star_vel, star_accel, star_mass, active, density, flow_in, field_in):
+
+    def _start_sites(mesh_ax, buf):
+        found_now = all_gather(buf, mesh_ax)
+        b_now = jnp.sum(found_now, 0)
+        return b_now
+
     resident_total = star_pos.shape[1]
     old_acc = star_accel[0:3]
     old_jerk = star_accel[3:6]
@@ -142,7 +149,7 @@
     packed = jnp.dot(resident, selector, precision=highest)
     targets = lax.all_gather(packed, ("star", "gas"), axis=1, tiled=True)
     partial_terms, kick_sum = all_terms(targets, resident, cell_place, cell_mass)
-    summed = lax.psum(partial_terms, ("star", "gas"))
+    summed = _start_sites(("star", "gas"), partial_terms)
     mine_terms = lax.dynamic_slice_in_dim(summed, my_rank * MOST, MOST, 1)
     own_terms = jnp.dot(mine_terms, selector.T, precision=highest)
     new_acc = own_terms[0:3]

time: 1060 us -> 1590 us (1.50)
  waiting for transfers between devices: 235 us -> 741 us
  other arithmetic: 139 us -> 157 us
    all_gather x0 -> x1, waiting for transfers between devices: none -> 737 us  [_start_sites(): found_now = all_gather(buf, mesh_ax)]
    psum x1 -> x0, waiting for transfers between devices: 231 us -> none  [body(): summed = lax.psum(partial_terms, ('star', 'gas'))]
    reduce_sum x0 -> x1, other arithmetic: none -> 17.7 us  [_start_sites(): b_now = jnp.sum(found_now, 0)]
  transfers between devices with their start and end apart: 9 -> 9, of which waited for: 3 -> 6; matrix products, arithmetic and copies ran while one was open for 0% -> 0% of each run, Pallas kernels for 0% -> 0%
where the time goes in v1:
time: 1590 us; the launch traced here: 1580 us
  waiting for transfers between devices  741 us (47%)
  blocking collectives  629 us (40%)
  other arithmetic  157 us (10%)
  starting transfers between devices  23.5 us (1%)
    all_gather x1, waiting for transfers between devices, _start_sites(): found_now = all_gather(buf, mesh_ax)  737 us
    all_gather x1, blocking collectives, body(): targets = lax.all_gather(packed, ('star', 'gas'), axis=1, tiled=True)  629 us
    reduce_sum x96, other arithmetic, pair_terms(): gas_acc = jnp.sum((inv_cube * cell_mass[None, :])[None] * cell_gap, 2)  48.2 us
  transfers between devices with their start and end apart: 9, of which 6 were waited for; matrix products, arithmetic and copies ran while one was open for 0% of the time, Pallas kernels for 0%

profile of v1, /device:TPU:1, one launch (start us, length us, event | category | flops | bytes accessed | tf_op | source)
XLA Modules:
  0.0 1583.9 jit_solution(17852836197925867691)
XLA Ops:
  7.3 0.7 add_select_fusion
  8.0 0.8 mul.753
  8.8 0.7 convert_bitcast_fusion
  10.3 0.8 multiply_add_fusion.8
  11.2 1.4 fusion.14
  12.7 629.3 %all-gather = f32[256,24,7]{1,2,0:T(8,128)S(1)} all-gather(f32[1,24,7]{1,2,0:T(8,128)S(1)} %convolution_bitcast_fusion), channel_id=1, replica_groups=mesh['star'=64,'gas'=4] {'star','gas'}, dimensions={0}, use_global_device_ids=true | all-gather | bytes 172704 | tf_op jit(solution)/shard_map/all_gather | solution.py:150
  642.2 0.5 reshape.155
  642.8 145.6 %while.14 = (s32[]{:T(128)}, f32[3,2048]{1,0:T(4,128)S(1)}, f32[96,6,64]{2,1,0:T(8,128)S(1)}, f32[3,4,8,64]{3,2,1,0:T(8,128)}, f32[96,7,64]{2,0,1:T(8,128)S(1)},...) while((s32[]{:T(128)}, f32[3,2048]{1,0:T(4,128)S(1)}, ...), condition=%wide.wide.region_11.12_spmd.clone, body=%wide.wide.region_3.11_spmd.clone.sunk | while | flops 5353989 | bytes 4405195 | solution.py:103
  643.8 0.5 fusion.148
  645.3 0.5 fusion.148
  646.8 0.5 fusion.148
  648.3 0.5 fusion.148
  649.9 0.5 fusion.148
  651.4 0.5 fusion.148
  652.9 0.5 fusion.148
  654.4 0.5 fusion.148
  655.9 0.5 fusion.148
  657.4 0.5 fusion.148
  659.0 0.5 fusion.148
  660.5 0.5 fusion.148
  662.0 0.5 fusion.148
  663.5 0.5 fusion.148
  665.0 0.5 fusion.148
  666.5 0.5 fusion.148
  668.1 0.5 fusion.148
  671.1 0.5 fusion.148
  672.6 0.5 fusion.148
  674.1 0.5 fusion.148
  675.6 0.5 fusion.148
  677.2 0.5 fusion.148
  678.7 0.5 fusion.148
  680.2 0.5 fusion.148
  681.7 0.5 fusion.148
  683.2 0.5 fusion.148
  684.7 0.5 fusion.148
  788.6 0.8 all_gather_reshape.3
  789.7 6.9 collective-permute-start.1
  796.5 0.6 collective-permute-done
  797.6 3.6 collective-permute-start.3
  801.1 1.6 collective-permute-done.2
  804.0 8.9 collective-permute-start.5
  812.9 0.8 convert_reduce_fusion
  814.0 3.7 collective-permute-start.7
  817.7 2.0 collective-permute-done.6
  821.0 0.6 fusion.58
  821.6 736.9 %all-gather.3.cloned.1.call-done = f32[256,6,6144]{2,1,0:T(8,128)} async-done(((f32[1,6,6144]{2,1,0:T(8,128)}), f32[256,6,6144]{2,1,0:T(8,128)}) %all-gather.3.cloned.1.call-update) | async-done | bytes 37748752 | tf_op jit(solution)/shard_map/all_gather | solution.py:110
  1558.5 17.7 %reduce_sum.82 = f32[6,6144]{1,0:T(8,128)S(1)} reduce(f32[256,6,6144]{2,1,0:T(8,128)} %all-gather.3.cloned.1.call-done, f32[]{:T(128)} %constant.94.clone.1), dimensions={0}, to_apply=%region_12.13 | reduce | flops 9400320 | bytes 37896196 | tf_op jit(solution)/shard_map/reduce_sum | solution.py:111
  1576.4 0.6 maximum_select_fusion
  (1312 shorter events, 127.6 us)
Async XLA Ops:
  7.2 1551.3 %all-gather.3.cloned.1.call-start = ((), (), s32[]{:S(2)}) async-start(), calls=%async_computation | async-start | bytes 50528256 | tf_op jit(solution)/shard_map/all_gather | solution.py:110
  7.3 5.3 copy-start.5
  10.2 631.7 %copy-start.3 = (f32[3,4,8,64]{3,2,1,0:T(8,128)}, f32[3,4,8,64]{3,2,1,0:T(8,128)S(1)}, u32[]{:S(2)}) copy-start(f32[3,4,8,64]{3,2,1,0:T(8,128)S(1)} %pad_maximum_fusion.20) | copy-start | bytes 73732
  642.8 146.7 %copy-start.8 = (f32[3,4,8,64]{3,2,1,0:T(8,128)S(1)}, f32[3,4,8,64]{3,2,1,0:T(8,128)}, u32[]{:S(2)}) copy-start(f32[3,4,8,64]{3,2,1,0:T(8,128)} %param.16) | copy-start | bytes 73732
  788.5 1.0 copy-start.1
  788.5 1.0 copy-start.2
  789.5 30.2 %copy-start = (f32[3,4,8,64]{3,2,1,0:T(8,128)}, f32[3,4,8,64]{3,2,1,0:T(8,128)S(1)}, u32[]{:S(2)}) copy-start(f32[3,4,8,64]{3,2,1,0:T(8,128)S(1)} %add.172) | copy-start | bytes 73732
  789.6 7.6 collective-permute-start
  789.7 7.8 collective-permute-start.1
  797.5 5.2 collective-permute-start.2
  797.6 5.1 collective-permute-start.3
  803.9 9.8 collective-permute-start.4
  804.0 9.8 collective-permute-start.5
  813.9 5.9 collective-permute-start.6
  814.0 5.8 collective-permute-start.7
  821.6 754.7 %copy-start.4 = (f32[6,512]{1,0:T(8,128)S(1)}, f32[6,512]{1,0:T(8,128)}, u32[]{:S(2)}) copy-start(f32[6,512]{1,0:T(8,128)} %param.12) | copy-start | bytes 36868
  821.6 754.7 %copy-start.6 = (f32[3,512]{1,0:T(4,128)S(1)}, f32[3,512]{1,0:T(4,128)}, u32[]{:S(2)}) copy-start(f32[3,512]{1,0:T(4,128)} %param.10) | copy-start | bytes 18436
  821.6 754.7 %copy-start.7 = (f32[3,512]{1,0:T(4,128)S(1)}, f32[3,512]{1,0:T(4,128)}, u32[]{:S(2)}) copy-start(f32[3,512]{1,0:T(4,128)} %param.11) | copy-start | bytes 18436
Sparse Core Ops, SparseCore 0:
  789.5 768.9 all-gather.2
